TPU v7x, 32 devices: a whole 2x2x4 slice. The times are simulated.
32 devices in a mesh: seq: 8 (over z, y), wsh: 4 (over x, core).
Axes of the slice: x: 2, y: 2, z: 4, core: 2. Of those that a mesh axis runs over, the one named last changes fastest.
Arguments:
- layer_input: bfloat16 [4096, 1152], P(('seq', 'wsh')), may hold values from -6 to 6
- w_qkv: bfloat16 [1152, 1536], P('wsh'), may hold values from -0.1875 to 0.1875
- w_out: bfloat16 [1152, 1024], P('wsh'), may hold values from -0.1875 to 0.1875
- w_gate_up: bfloat16 [1152, 6912], P('wsh'), may hold values from -0.1875 to 0.1875
- w_down: bfloat16 [1152, 3456], P('wsh'), may hold values from -0.109375 to 0.109375
- norm_gain: bfloat16 [4, 1152], P(None, 'wsh'), may hold values from 0.099609375 to 1.8984375
- qk_gain: bfloat16 [512], P('wsh'), may hold values from 0.099609375 to 1.8984375
- cotangent: bfloat16 [4096, 1152], P(('seq', 'wsh')), may hold values from -6 to 6
Outputs:
- output: bfloat16 [4096, 1152], P(('seq', 'wsh'))
- grad_input: float32 [4096, 1152], P(('seq', 'wsh'))
- grad_w_qkv: float32 [1152, 1536], P('wsh')
- grad_w_out: float32 [1152, 1024], P('wsh')
- grad_w_gate_up: float32 [1152, 6912], P('wsh')
- grad_w_down: float32 [1152, 3456], P('wsh')
- grad_norm_gain: float32 [4, 1152], P(None, 'wsh')
- grad_qk_gain: float32 [512], P('wsh')
All inputs are finite; a program needn't handle non-finite values.
Results may differ from a plain program's by a relative error of at most 0.024.
Values may be sent and summed in bfloat16 or wider, within the bound.
No kernel may reach another device: no remote copies, remote signals or barrier semaphores. Data moves between devices by JAX's collectives and lax.ppermute only.
A program may use at most 192 MiB of HBM per device.

v0:
```python
import jax
import jax.numpy as jnp
from jax import lax
from jax.sharding import PartitionSpec as P

WIN = 512
EPSILON = 1e-06
GELU_COEF = 0.7978845608028654


def from_behind(value, axis, by):
    peers = lax.axis_size(axis)
    pairs = [(i, i + by) for i in range(peers) if 0 <= i + by < peers]
    return lax.ppermute(value, axis, pairs)


def gelu_tanh(values):
    return (
        0.5 * values * (1.0 + jnp.tanh(GELU_COEF * (values + 0.044715 * values * values * values)))
    )


def gelu_slope(values):
    bend = jnp.tanh(GELU_COEF * (values + 0.044715 * values * values * values))
    return 0.5 * (1.0 + bend) + 0.5 * values * (1.0 - bend * bend) * GELU_COEF * (
        1.0 + 3.0 * 0.044715 * values * values
    )


def inv_rms(values):
    return lax.rsqrt(jnp.mean(values * values, -1, keepdims=True) + EPSILON)


def norm_back(grad_out, values, scale, gain):
    normed = values * scale
    scaled = grad_out * gain
    grad_in = scale * (scaled - normed * jnp.mean(scaled * normed, -1, keepdims=True))
    return (grad_in, grad_out * normed)


def rope_tables(positions, head_dim):
    half = head_dim // 2
    freqs = 10000.0 ** (-(jnp.arange(half, dtype=jnp.float32) * 2.0 / head_dim))
    angles = positions.astype(jnp.float32)[:, None] * freqs[None, :]
    cosine = jnp.cos(angles)
    sine = jnp.sin(angles)
    return (jnp.concatenate([cosine, cosine], -1), jnp.concatenate([sine, sine], -1))


def rotate(values, cosine, sine):
    half = values.shape[-1] // 2
    turned = jnp.concatenate([-values[..., half:], values[..., :half]], -1)
    return values * cosine + turned * sine


def unrotate(grads, cosine, sine):
    half = grads.shape[-1] // 2
    scaled = grads * sine
    turned = jnp.concatenate([scaled[..., half:], -scaled[..., :half]], -1)
    return grads * cosine + turned


def block_mask(query_pos, key_pos):
    gap = query_pos[:, None] - key_pos[None, :]
    return (gap >= 0) & (gap < WIN) & (key_pos[None, :] >= 0)


def outer_sum(left, right):
    return lax.dot_general(
        left, right, (((0,), (0,)), ((), ())), preferred_element_type=jnp.float32
    )


def attend(query_s, keys, mask):
    head_dim = query_s.shape[-1]
    scores = jnp.einsum(
        "qhd,kd->hqk", query_s, keys[:, :head_dim], preferred_element_type=jnp.float32
    )
    exps = jnp.where(mask[None], jnp.exp(scores), 0.0)
    total = jnp.sum(exps, -1, keepdims=True)
    weights = (exps / total).astype(jnp.bfloat16)
    out = jnp.einsum("hqk,kd->qhd", weights, keys[:, head_dim:], preferred_element_type=jnp.float32)
    return (out, jnp.log(total))


def attend_back(query_s, keys, mask, out, log_total, grad_out):
    head_dim = query_s.shape[-1]
    scores = jnp.einsum(
        "qhd,kd->hqk", query_s, keys[:, :head_dim], preferred_element_type=jnp.float32
    )
    probs = jnp.where(mask[None], jnp.exp(scores - log_total), 0.0)
    grad_prob = jnp.einsum(
        "qhd,kd->hqk", grad_out, keys[:, head_dim:], preferred_element_type=jnp.float32
    )
    delta = jnp.einsum("qhd,qhd->hq", grad_out.astype(jnp.float32), out)[:, :, None]
    grad_score = (probs * (grad_prob - delta)).astype(jnp.bfloat16)
    grad_query = jnp.einsum(
        "hqk,kd->qhd", grad_score, keys[:, :head_dim], preferred_element_type=jnp.float32
    )
    grad_key = jnp.einsum("hqk,qhd->kd", grad_score, query_s, preferred_element_type=jnp.float32)
    grad_value = jnp.einsum(
        "hqk,qhd->kd", probs.astype(jnp.bfloat16), grad_out, preferred_element_type=jnp.float32
    )
    return (grad_query, jnp.concatenate([grad_key, grad_value], -1))


def body(layer_input, w_qkv, w_out, w_gate_up, w_down, norm_gain, qk_gain, cotangent):
    wsh_count = lax.axis_size("wsh")
    seq_index = lax.axis_index("seq")
    wsh_index = lax.axis_index("wsh")
    rows = layer_input.shape[0]
    block = rows * wsh_count
    gathered = (
        lax.all_gather(w_qkv, "wsh", axis=0, tiled=True),
        lax.all_gather(w_out, "wsh", axis=0, tiled=True),
        lax.all_gather(w_gate_up, "wsh", axis=0, tiled=True),
        lax.all_gather(w_down, "wsh", axis=0, tiled=True),
        lax.all_gather(norm_gain, "wsh", axis=1, tiled=True),
        lax.all_gather(qk_gain, "wsh", axis=0, tiled=True),
    )
    qkv_full, out_full, gate_up_full, down_full, norm_full, qk_full = gathered
    gains = norm_full.astype(jnp.float32)
    head_dim = qk_full.shape[0] // 2
    heads = out_full.shape[1] // head_dim
    width_q = heads * head_dim
    hidden_units = down_full.shape[1]
    gain_query = qk_full[:head_dim].astype(jnp.float32)
    gain_key = qk_full[head_dim:].astype(jnp.float32)
    own_start = (seq_index * wsh_count + wsh_index) * rows
    positions = own_start + jnp.arange(rows, dtype=jnp.int32)
    key_pos = own_start - WIN + jnp.arange(WIN + rows, dtype=jnp.int32)
    mask = block_mask(positions, key_pos)
    cosine, sine = rope_tables(positions, head_dim)
    rows_f = layer_input.astype(jnp.float32)
    scale1 = inv_rms(rows_f)
    normed = (rows_f * scale1 * gains[0]).astype(jnp.bfloat16)
    projected = jnp.dot(normed, qkv_full, preferred_element_type=jnp.float32)
    query = projected[:, :width_q].reshape(rows, heads, head_dim)
    key = projected[:, width_q : width_q + head_dim]
    value = projected[:, width_q + head_dim :]
    scale_q = inv_rms(query)
    scale_k = inv_rms(key)
    query_s = (
        rotate(query * scale_q * gain_query, cosine[:, None], sine[:, None]) * head_dim ** (-0.5)
    ).astype(jnp.bfloat16)
    key_s = rotate(key * scale_k * gain_key, cosine, sine).astype(jnp.bfloat16)
    local_kv = jnp.concatenate([key_s, value.astype(jnp.bfloat16)], -1)
    block_kv = lax.all_gather(local_kv, "wsh", axis=0, tiled=True)
    previous = from_behind(block_kv, "seq", 1)
    keys = lax.dynamic_slice_in_dim(
        jnp.concatenate([previous, block_kv], 0), wsh_index * rows, WIN + rows, 0
    )
    attended, log_total = attend(query_s, keys, mask)
    attended_b = attended.reshape(rows, width_q).astype(jnp.bfloat16)
    branch = lax.dot_general(
        attended_b, out_full, (((1,), (1,)), ((), ())), preferred_element_type=jnp.float32
    )
    scale2 = inv_rms(branch)
    hidden_res = rows_f + branch * scale2 * gains[1]
    scale3 = inv_rms(hidden_res)
    ffn_in = (hidden_res * scale3 * gains[2]).astype(jnp.bfloat16)
    gate_up = jnp.dot(ffn_in, gate_up_full, preferred_element_type=jnp.float32)
    gate = gate_up[:, :hidden_units]
    upper = gate_up[:, hidden_units:]
    mixed = (gelu_tanh(gate) * upper).astype(jnp.bfloat16)
    ffn_out = lax.dot_general(
        mixed, down_full, (((1,), (1,)), ((), ())), preferred_element_type=jnp.float32
    )
    scale4 = inv_rms(ffn_out)
    output = (hidden_res + ffn_out * scale4 * gains[3]).astype(jnp.bfloat16)
    gathered = (
        lax.all_gather(w_qkv, "wsh", axis=0, tiled=True),
        lax.all_gather(w_out, "wsh", axis=0, tiled=True),
        lax.all_gather(w_gate_up, "wsh", axis=0, tiled=True),
        lax.all_gather(w_down, "wsh", axis=0, tiled=True),
        lax.all_gather(norm_gain, "wsh", axis=1, tiled=True),
        lax.all_gather(qk_gain, "wsh", axis=0, tiled=True),
    )
    qkv_full, out_full, gate_up_full, down_full, norm_full, qk_full = gathered
    gains = norm_full.astype(jnp.float32)
    gain_query = qk_full[:head_dim].astype(jnp.float32)
    gain_key = qk_full[head_dim:].astype(jnp.float32)
    grad_y = cotangent.astype(jnp.float32)
    grad_ffn, rows_three = norm_back(grad_y, ffn_out, scale4, gains[3])
    grad_ffn_b = grad_ffn.astype(jnp.bfloat16)
    grad_mixed = jnp.dot(grad_ffn_b, down_full, preferred_element_type=jnp.float32)
    grad_gu = jnp.concatenate(
        [grad_mixed * upper * gelu_slope(gate), grad_mixed * gelu_tanh(gate)], -1
    ).astype(jnp.bfloat16)
    grad_ffn_in = lax.dot_general(
        grad_gu, gate_up_full, (((1,), (1,)), ((), ())), preferred_element_type=jnp.float32
    )
    grad_res, rows_two = norm_back(grad_ffn_in, hidden_res, scale3, gains[2])
    grad_hidden = grad_y + grad_res
    grad_branch, rows_one = norm_back(grad_hidden, branch, scale2, gains[1])
    grad_branch_b = grad_branch.astype(jnp.bfloat16)
    grad_att = (
        jnp.dot(grad_branch_b, out_full, preferred_element_type=jnp.float32)
        .astype(jnp.bfloat16)
        .reshape(rows, heads, head_dim)
    )
    grad_query, grad_keys = attend_back(query_s, keys, mask, attended, log_total, grad_att)
    spread = lax.dynamic_update_slice_in_dim(
        jnp.zeros((WIN + block, 2 * head_dim), jnp.float32), grad_keys, wsh_index * rows, 0
    )
    returned = from_behind(spread[:WIN].astype(jnp.bfloat16), "seq", -1).astype(jnp.float32)
    own_part = spread[WIN:]
    own_part = jnp.concatenate([own_part[: block - WIN], own_part + returned], 0)
    grad_kv = lax.psum_scatter(
        own_part.astype(jnp.bfloat16), "wsh", scatter_dimension=0, tiled=True
    ).astype(jnp.float32)
    grad_qn = unrotate(grad_query, cosine[:, None], sine[:, None]) * head_dim ** (-0.5)
    grad_q, rows_query = norm_back(grad_qn, query, scale_q, gain_query)
    grad_kn = unrotate(grad_kv[:, :head_dim], cosine, sine)
    grad_k, rows_key = norm_back(grad_kn, key, scale_k, gain_key)
    grad_qkv = jnp.concatenate(
        [grad_q.reshape(rows, width_q), grad_k, grad_kv[:, head_dim:]], -1
    ).astype(jnp.bfloat16)
    grad_normed = lax.dot_general(
        grad_qkv, qkv_full, (((1,), (1,)), ((), ())), preferred_element_type=jnp.float32
    )
    grad_in, rows_zero = norm_back(grad_normed, rows_f, scale1, gains[0])
    grad_input = grad_hidden + grad_in
    gain_grads = jnp.stack(
        [jnp.sum(rows_zero, 0), jnp.sum(rows_one, 0), jnp.sum(rows_two, 0), jnp.sum(rows_three, 0)]
    )
    qk_grads = jnp.concatenate([jnp.sum(rows_query, (0, 1)), jnp.sum(rows_key, 0)], 0)
    terms = (
        outer_sum(normed, grad_qkv),
        outer_sum(grad_branch_b, attended_b),
        outer_sum(ffn_in, grad_gu),
        outer_sum(grad_ffn_b, mixed),
        gain_grads,
        qk_grads,
    )
    owned = (
        lax.psum_scatter(
            terms[0].astype(jnp.bfloat16), "wsh", scatter_dimension=0, tiled=True
        ).astype(jnp.float32),
        lax.psum_scatter(
            terms[1].astype(jnp.bfloat16), "wsh", scatter_dimension=0, tiled=True
        ).astype(jnp.float32),
        lax.psum_scatter(
            terms[2].astype(jnp.bfloat16), "wsh", scatter_dimension=0, tiled=True
        ).astype(jnp.float32),
        lax.psum_scatter(
            terms[3].astype(jnp.bfloat16), "wsh", scatter_dimension=0, tiled=True
        ).astype(jnp.float32),
        lax.psum_scatter(
            terms[4].astype(jnp.bfloat16), "wsh", scatter_dimension=1, tiled=True
        ).astype(jnp.float32),
        lax.psum_scatter(
            terms[5].astype(jnp.bfloat16), "wsh", scatter_dimension=0, tiled=True
        ).astype(jnp.float32),
    )
    grads = (
        lax.psum(owned[0].astype(jnp.bfloat16), "seq").astype(jnp.float32),
        lax.psum(owned[1].astype(jnp.bfloat16), "seq").astype(jnp.float32),
        lax.psum(owned[2].astype(jnp.bfloat16), "seq").astype(jnp.float32),
        lax.psum(owned[3].astype(jnp.bfloat16), "seq").astype(jnp.float32),
        lax.psum(owned[4].astype(jnp.bfloat16), "seq").astype(jnp.float32),
        lax.psum(owned[5].astype(jnp.bfloat16), "seq").astype(jnp.float32),
    )
    return (output, grad_input, grads[0], grads[1], grads[2], grads[3], grads[4], grads[5])


def solution(mesh):
    in_specs = (
        P(("seq", "wsh"), None),
        P("wsh", None),
        P("wsh", None),
        P("wsh", None),
        P("wsh", None),
        P(None, "wsh"),
        P("wsh"),
        P(("seq", "wsh"), None),
    )
    out_specs = (
        P(("seq", "wsh"), None),
        P(("seq", "wsh"), None),
        P("wsh", None),
        P("wsh", None),
        P("wsh", None),
        P("wsh", None),
        P(None, "wsh"),
        P("wsh"),
    )
    return jax.shard_map(body, mesh=mesh, in_specs=in_specs, out_specs=out_specs, check_vma=False)
```

profile of v0, /device:TPU:0, one launch (start us, length us, event | category | flops | bytes accessed | tf_op | source)
XLA Modules:
  0.0 865.7 jit_solution(17018947005329664847)
XLA Ops:
  10.1 6.2 all-gather
  16.4 5.3 all-gather.1
  22.6 20.4 %all-gather.7.cloned.1.call-done = bf16[1152,1536]{1,0:T(8,128)(2,1)} async-done(((bf16[288,1536]{1,0:T(8,128)(2,1)}), bf16[1152,1536]{1,0:T(8,128)(2,1)}) %all-gather.7.cloned.1.call-update) | async-done | bytes 3538960 | tf_op jit(solution)/shard_map/all_gather | solution.py:114
  43.0 2.7 fusion.50
  47.0 7.2 all_gather.30
  54.2 3.6 collective-permute-start
  58.4 10.9 %collective-permute-done = bf16[512,512]{1,0:T(8,128)(2,1)S(1)} collective-permute-done((bf16[512,512]{1,0:T(8,128)(2,1)S(1)}, bf16[512,512]{1,0:T(8,128)(2,1)S(1)}, u32[]{:S(2)}, u32[]{:S(2)}) %collective-permute-start) | collective-permute-done | bytes 524320 | tf_op jit(solution)/shard_map/ppermute | solution.py:14
  71.5 1.3 bitcast_convert_fusion
  72.8 2.7 multiply_reduce_fusion.6
  75.9 95.5 %all-gather.11.cloned.1.call-done = bf16[1152,6912]{1,0:T(8,128)(2,1)} async-done(((bf16[288,6912]{1,0:T(8,128)(2,1)}), bf16[1152,6912]{1,0:T(8,128)(2,1)}) %all-gather.11.cloned.1.call-update) | async-done | bytes 15925264 | tf_op jit(solution)/shard_map/all_gather | solution.py:116
  171.3 8.0 fusion.59
  179.4 1.8 copy-done
  181.8 46.8 %all-gather.13.cloned.1.call-done = bf16[1152,3456]{1,0:T(8,128)(2,1)} async-done(((bf16[288,3456]{1,0:T(8,128)(2,1)}), bf16[1152,3456]{1,0:T(8,128)(2,1)}) %all-gather.13.cloned.1.call-update) | async-done | bytes 7962640 | tf_op jit(solution)/shard_map/all_gather | solution.py:117
  228.6 6.0 multiply_reduce_fusion.4
  235.5 1.0 fusion.29
  236.4 3.4 fusion.6
  239.8 12.7 %multiply_reduce_fusion = (bf16[1152]{0:T(1024)(128)(2,1)}, f32[128]{0:T(128)S(1)}, f32[128,1152]{1,0:T(8,128)}) fusion(f32[128,1152]{1,0:T(8,128)S(1)} %get-tuple-element.33, f32[128]{0:T(128)S(1)} %add_rsqrt_fusion.2, f32[1152]{0:T(1024)S(1)} %get-tuple-element.21, bf16[1152,6912]{1,0:T(8,128)(2,1)} %all-gather.11.cloned.1.call-done, ...), kind=kOutput, calls=%fused_computation.67 | convolution fusion | flops 2042854144 | bytes 18882304 | tf_op jit(solution)/shard_map/dot_general | solution.py:190
  252.6 2.3 multiply_reduce_fusion.1
  258.2 1.2 copy.113
  259.5 1.9 convolution_bitcast_fusion.2
  261.4 1.1 fusion.41
  264.4 1.4 collective-permute-start.1
  265.9 14.7 %collective-permute-done.1 = bf16[512,512]{1,0:T(8,128)(2,1)S(1)} collective-permute-done((bf16[512,512]{1,0:T(8,128)(2,1)S(1)}, bf16[512,512]{1,0:T(8,128)(2,1)S(1)}, u32[]{:S(2)}, u32[]{:S(2)}) %collective-permute-start.1) | collective-permute-done | bytes 524320 | tf_op jit(solution)/shard_map/ppermute | solution.py:14
  280.5 1.0 fusion.13
  281.6 2.3 convolution_convert_fusion.3
  285.0 1.4 broadcast_multiply_fusion
  286.9 16.5 %reduce-scatter.9.cloned.1.call-done = bf16[128,512]{1,0:T(8,128)(2,1)} async-done(((bf16[512,512]{1,0:T(8,128)(2,1)}), bf16[128,512]{1,0:T(8,128)(2,1)}) %reduce-scatter.9.cloned.1.call-update) | async-done | bytes 131088 | tf_op jit(solution)/shard_map/reduce_scatter | solution.py:209
  305.2 1.1 multiply_reduce_fusion.10
  306.3 1.0 multiply_convert_fusion.5
  307.5 3.0 convolution_convert_fusion.2
  311.5 5.5 convolution_convert_fusion.1
  317.1 1.1 copy-done.7
  318.2 9.1 %convolution_convert_fusion = bf16[1152,6912]{1,0:T(8,128)(2,1)} fusion(bf16[128,3456]{1,0:T(8,128)(2,1)} %get-tuple-element.35, bf16[128,3456]{1,0:T(8,128)(2,1)S(1)} %copy-done.7, f32[128,1152]{1,0:T(8,128)S(1)} %get-tuple-element.33, f32[1152]{0:T(1024)S(1)} %get-tuple-element.21, f32[128]{0:T(128)S(1)} %copy-done.39), kind=kOutput, calls=%fused_computation | convolution fusion | flops 2050375680 | bytes 18289664 | tf_op jit(solution)/shard_map/dot_general | solution.py:69
  328.1 3.4 fusion.35
  332.5 6.1 reduce-scatter.13.cloned.1.call-done
  338.6 43.5 %reduce-scatter.11.cloned.1.call-done = bf16[288,1536]{1,0:T(8,128)(2,1)} async-done(((bf16[1152,1536]{1,0:T(8,128)(2,1)}), bf16[288,1536]{1,0:T(8,128)(2,1)}) %reduce-scatter.11.cloned.1.call-update) | async-done | bytes 884752 | tf_op jit(solution)/shard_map/reduce_scatter | solution.py:237
  382.1 72.1 %reduce-scatter.17.cloned.1.call-done = bf16[288,3456]{1,0:T(8,128)(2,1)} async-done(((bf16[1152,3456]{1,0:T(8,128)(2,1)}), bf16[288,3456]{1,0:T(8,128)(2,1)}) %reduce-scatter.17.cloned.1.call-update) | async-done | bytes 1990672 | tf_op jit(solution)/shard_map/reduce_scatter | solution.py:246
  454.2 122.7 %reduce-scatter.15.cloned.1.call-done = bf16[288,6912]{1,0:T(8,128)(2,1)} async-done(((bf16[1152,6912]{1,0:T(8,128)(2,1)}), bf16[288,6912]{1,0:T(8,128)(2,1)}) %reduce-scatter.15.cloned.1.call-update) | async-done | bytes 3981328 | tf_op jit(solution)/shard_map/reduce_scatter | solution.py:243
  578.8 5.8 all-reduce
  584.6 1.0 fusion.34
  585.7 14.4 %reduce-scatter.19.cloned.1.call-done = bf16[288,4]{1,0:T(8,128)(2,1)} async-done(((bf16[1152,4]{1,0:T(8,128)(2,1)}), bf16[288,4]{1,0:T(8,128)(2,1)}) %reduce-scatter.19.cloned.1.call-update) | async-done | bytes 2320
  600.0 1.0 copy.125
  601.0 22.0 %all-reduce.1 = (bf16[4,288]{1,0:T(4,128)(2,1)S(1)}, bf16[128]{0:T(256)(128)(2,1)S(1)}) all-reduce(bf16[4,288]{1,0:T(4,128)(2,1)S(1)} %copy.125, bf16[128]{0:T(256)(128)(2,1)S(1)} %dynamic-slice.1), channel_id=1, replica_groups=mesh['seq'=8,'wsh'=4] {'seq'}, use_global_device_ids=true, to_apply=%region_27.28 | all-reduce | flops 1280 | bytes 5120 | tf_op jit(solution)/shard_map/psum | solution.py:261
  624.1 224.1 %all-reduce.5.cloned.1.call-done = (bf16[288,1536]{1,0:T(8,128)(2,1)}, bf16[288,1024]{1,0:T(8,128)(2,1)}, bf16[288,6912]{1,0:T(8,128)(2,1)}, bf16[288,3456]{1,0:T(8,128)(2,1)}) async-done(((bf16[288,1536]{1,0:T(8,128)(2,1)}, bf16[288,1024]{1,0:T(8,128)(2,1)}, bf16[288,6912]{1,0:T(8,128)(2,1)}, bf16[288,3456]{1,0:T(8,128)(2,1)}), (bf16[288,1536]{1,0:T(8,128)(2,1)}, bf16[288,1024]{1,0:T(8,128)(2,1)}, ...) | async-done | bytes 7446544 | tf_op jit(solution)/shard_map/psum | solution.py:257
  848.3 2.7 convert_element_type.146
  851.0 2.2 convert_element_type.148
  853.2 3.8 convert_element_type.150
  857.0 2.2 convert_element_type.152
  (199 shorter events, 23.2 us)
Async XLA Ops:
  7.2 35.9 %all-gather.7.cloned.1.call-start = ((), (), s32[]{:S(2)}) async-start(), calls=%async_computation.6 | async-start | bytes 4423680 | tf_op jit(solution)/shard_map/all_gather | solution.py:114
  7.9 64.9 %all-gather.9.cloned.1.call-start = ((), (), s32[]{:S(2)}) async-start(), calls=%async_computation.7 | async-start | bytes 2949120 | tf_op jit(solution)/shard_map/all_gather | solution.py:115
  8.7 162.7 %all-gather.11.cloned.1.call-start = ((), (), s32[]{:S(2)}) async-start(), calls=%async_computation.8 | async-start | bytes 19906560 | tf_op jit(solution)/shard_map/all_gather | solution.py:116
  9.4 7.0 copy-start.49
  9.4 12.4 %copy-start.4 = (bf16[128,1152]{1,0:T(8,128)(2,1)S(1)}, bf16[128,1152]{1,0:T(8,128)(2,1)}, u32[]{:S(2)}) copy-start(bf16[128,1152]{1,0:T(8,128)(2,1)} %param.8) | copy-start | bytes 884740
  9.4 219.2 %all-gather.13.cloned.1.call-start = ((), (), s32[]{:S(2)}) async-start(), calls=%async_computation.9 | async-start | bytes 9953280 | tf_op jit(solution)/shard_map/all_gather | solution.py:117
  10.0 293.4 %reduce-scatter.9.cloned.1.call-start = ((), (), s32[]{:S(2)}) async-start(), calls=%async_computation.10 | async-start | bytes 655360 | tf_op jit(solution)/shard_map/reduce_scatter | solution.py:209
  22.0 23.8 %copy-start.46 = (f32[128]{0:T(128)}, f32[128]{0:T(128)S(1)}, u32[]{:S(2)}) copy-start(f32[128]{0:T(128)S(1)} %add_rsqrt_fusion.5) | copy-start | bytes 1540
  22.0 24.9 %copy-start.36 = (f32[2,1,128]{2,1,0:T(1,128)}, f32[2,1,128]{2,1,0:T(1,128)S(1)}, u32[]{:S(2)}) copy-start(f32[2,1,128]{2,1,0:T(1,128)S(1)} %get-tuple-element.49) | copy-start | bytes 3076
  22.0 36.2 %copy-start.43 = (f32[2,1,128]{2,1,0:T(1,128)}, f32[2,1,128]{2,1,0:T(1,128)S(1)}, u32[]{:S(2)}) copy-start(f32[2,1,128]{2,1,0:T(1,128)S(1)} %get-tuple-element.50) | copy-start | bytes 3076
  22.2 48.3 %copy-start.32 = (pred[128,640]{0,1:T(8,128)(4,1)}, pred[128,640]{0,1:T(8,128)(4,1)S(1)}, u32[]{:S(2)}) copy-start(pred[128,640]{0,1:T(8,128)(4,1)S(1)} %fusion.43) | copy-start | bytes 245764
  22.6 24.3 %copy-start.23 = (f32[128,128]{1,0:T(8,128)}, f32[128,128]{1,0:T(8,128)S(1)}, u32[]{:S(2)}) copy-start(f32[128,128]{1,0:T(8,128)S(1)} %get-tuple-element.51) | copy-start | bytes 196612
  22.6 24.3 %copy-start.30 = (f32[128,128]{1,0:T(8,128)}, f32[128,128]{1,0:T(8,128)S(1)}, u32[]{:S(2)}) copy-start(f32[128,128]{1,0:T(8,128)S(1)} %get-tuple-element.52) | copy-start | bytes 196612
  46.7 11.4 %copy-start.44 = (f32[128]{0:T(128)}, f32[128]{0:T(128)S(1)}, u32[]{:S(2)}) copy-start(f32[128]{0:T(128)S(1)} %add_rsqrt_fusion.4) | copy-start | bytes 1540
  54.2 15.0 %collective-permute-start = (bf16[512,512]{1,0:T(8,128)(2,1)S(1)}, bf16[512,512]{1,0:T(8,128)(2,1)S(1)}, u32[]{:S(2)}, u32[]{:S(2)}) collective-permute-start(bf16[512,512]{1,0:T(8,128)(2,1)S(1)} %all_gather.30), channel_id=1, source_target_pairs={{0,4},{4,8},{8,12},{12,16},{16,20},{20,24},{24,28},{1,5},{5,9},{9,... | collective-permute-start | bytes 1572872 | tf_op jit(solution)/shard_map/ppermute | solution.py:14
  58.0 12.1 %copy-start.22 = (f32[128,256]{0,1:T(8,128)}, f32[128,256]{0,1:T(8,128)S(1)}, u32[]{:S(2)}) copy-start(f32[128,256]{0,1:T(8,128)S(1)} %copy.91) | copy-start | bytes 393220
  58.1 11.9 %copy-start.20 = (f32[128,256]{0,1:T(8,128)}, f32[128,256]{0,1:T(8,128)S(1)}, u32[]{:S(2)}) copy-start(f32[128,256]{0,1:T(8,128)S(1)} %copy.90) | copy-start | bytes 393220
  58.4 12.1 %copy-start.27 = (bf16[128,4,256]{0,2,1:T(8,128)(2,1)}, bf16[128,4,256]{0,2,1:T(8,128)(2,1)S(1)}, u32[]{:S(2)}) copy-start(bf16[128,4,256]{0,2,1:T(8,128)(2,1)S(1)} %fusion.40) | copy-start | bytes 786436
  72.8 3.0 copy-start.25
  75.9 176.7 %copy-start.38 = (f32[128]{0:T(128)}, f32[128]{0:T(128)S(1)}, u32[]{:S(2)}) copy-start(f32[128]{0:T(128)S(1)} %add_rsqrt_fusion.2) | copy-start | bytes 1540
  179.4 1.8 copy-start
  181.8 52.8 %copy-start.8 = (bf16[128,1152]{1,0:T(8,128)(2,1)S(1)}, bf16[128,1152]{1,0:T(8,128)(2,1)}, u32[]{:S(2)}) copy-start(bf16[128,1152]{1,0:T(8,128)(2,1)} %param.15) | copy-start | bytes 884740
  228.6 7.8 copy-start.1
  228.6 7.8 copy-start.3
  236.4 3.4 copy-start.14
  252.6 3.2 copy-start.2
  256.3 3.2 copy-start.33
  259.5 3.1 copy-start.17
  259.5 3.1 copy-start.19
  259.5 3.1 copy-start.29
  264.3 17.3 %copy-start.10 = (bf16[128,1152]{1,0:T(8,128)(2,1)S(1)}, bf16[128,1152]{1,0:T(8,128)(2,1)}, u32[]{:S(2)}) copy-start(bf16[128,1152]{1,0:T(8,128)(2,1)} %copy-done.9) | copy-start | bytes 884740
  264.4 17.3 %copy-start.26 = (bf16[128,4,256]{0,2,1:T(8,128)(2,1)S(1)}, bf16[128,4,256]{0,2,1:T(8,128)(2,1)}, u32[]{:S(2)}) copy-start(bf16[128,4,256]{0,2,1:T(8,128)(2,1)} %copy-done.25) | copy-start | bytes 786436
  264.4 16.1 %collective-permute-start.1 = (bf16[512,512]{1,0:T(8,128)(2,1)S(1)}, bf16[512,512]{1,0:T(8,128)(2,1)S(1)}, u32[]{:S(2)}, u32[]{:S(2)}) collective-permute-start(bf16[512,512]{1,0:T(8,128)(2,1)S(1)} %slice.205), channel_id=1, source_target_pairs={{4,0},{8,4},{12,8},{16,12},{20,16},{24,20},{28,24},{5,1},{9,5},{13... | collective-permute-start | bytes 1572872 | tf_op jit(solution)/shard_map/ppermute | solution.py:14
  281.5 57.0 %reduce-scatter.13.cloned.1.call-start = ((), (), s32[]{:S(2)}) async-start(), calls=%async_computation.12 | async-start | bytes 2949120 | tf_op jit(solution)/shard_map/reduce_scatter | solution.py:240
  283.9 98.2 %reduce-scatter.11.cloned.1.call-start = ((), (), s32[]{:S(2)}) async-start(), calls=%async_computation.11 | async-start | bytes 4423680 | tf_op jit(solution)/shard_map/reduce_scatter | solution.py:237
  284.0 2.5 copy-start.21
  284.0 2.5 copy-start.35
  286.5 17.9 %copy-start.31 = (f32[128,128]{1,0:T(8,128)S(1)}, f32[128,128]{1,0:T(8,128)}, u32[]{:S(2)}) copy-start(f32[128,128]{1,0:T(8,128)} %copy-done.30) | copy-start | bytes 196612
  286.5 18.7 %copy-start.24 = (f32[128,128]{1,0:T(8,128)S(1)}, f32[128,128]{1,0:T(8,128)}, u32[]{:S(2)}) copy-start(f32[128,128]{1,0:T(8,128)} %copy-done.23) | copy-start | bytes 196612
  286.5 18.7 %copy-start.37 = (f32[2,1,128]{2,1,0:T(1,128)S(1)}, f32[2,1,128]{2,1,0:T(1,128)}, u32[]{:S(2)}) copy-start(f32[2,1,128]{2,1,0:T(1,128)} %copy-done.36) | copy-start | bytes 3076
  286.5 18.7 %copy-start.45 = (f32[128]{0:T(128)S(1)}, f32[128]{0:T(128)}, u32[]{:S(2)}) copy-start(f32[128]{0:T(128)} %copy-done.44) | copy-start | bytes 1540
  286.7 20.8 %copy-start.47 = (f32[128]{0:T(128)S(1)}, f32[128]{0:T(128)}, u32[]{:S(2)}) copy-start(f32[128]{0:T(128)} %copy-done.46) | copy-start | bytes 1540
  310.5 143.7 %reduce-scatter.17.cloned.1.call-start = ((), (), s32[]{:S(2)}) async-start(), calls=%async_computation.14 | async-start | bytes 9953280 | tf_op jit(solution)/shard_map/reduce_scatter | solution.py:246
  317.0 259.8 %reduce-scatter.15.cloned.1.call-start = ((), (), s32[]{:S(2)}) async-start(), calls=%async_computation.13 | async-start | bytes 19906560 | tf_op jit(solution)/shard_map/reduce_scatter | solution.py:243
  327.4 272.6 %reduce-scatter.19.cloned.1.call-start = ((), (), s32[]{:S(2)}) async-start(), calls=%async_computation.15 | async-start | bytes 368640
  332.5 515.8 %all-reduce.5.cloned.1.call-start = ((), (), s32[]{:S(2)}) async-start(), calls=%async_computation.16 | async-start | bytes 14893056 | tf_op jit(solution)/shard_map/psum | solution.py:257
  848.3 4.9 copy-start.6
  853.2 3.8 copy-start.13
  (16 other events, 14.7 us)
Sparse Core Ops, SparseCore 0:
  9.5 33.4 all-gather.6
  44.6 24.0 all-gather.8
  70.2 101.0 all-gather.10
  172.7 55.8 all-gather.12
  281.7 21.6 reduce-scatter.8
  305.7 32.7 reduce-scatter.12
  341.7 40.3 reduce-scatter.10
  385.3 68.8 reduce-scatter.16
  456.8 120.0 reduce-scatter.14
  579.8 20.2 reduce-scatter.18
  604.6 243.6 all-reduce.4
where the time goes:
time: 867 us; the launch traced here: 866 us
  waiting for transfers between devices  690 us (80%)
  matrix products  65.2 us (8%)
  blocking collectives  46.5 us (5%)
  other arithmetic  27.9 us (3%)
  between operations  15.5 us (2%)
  local copies, waits for them, and re-layouts  15 us (2%)
    psum x1, waiting for transfers between devices, body(): lax.psum(owned[0].astype(jnp.bfloat16), 'seq').astype(jnp.float32)  224 us
    reduce_scatter x1, waiting for transfers between devices, body(): lax.psum_scatter(terms[2].astype(jnp.bfloat16), 'wsh', scatter_dimension=...  123 us
    all_gather x1, waiting for transfers between devices, body(): lax.all_gather(w_gate_up, 'wsh', axis=0, tiled=True)  95.5 us
    reduce_scatter x1, waiting for transfers between devices, body(): lax.psum_scatter(terms[3].astype(jnp.bfloat16), 'wsh', scatter_dimension=...  72.1 us
    all_gather x1, waiting for transfers between devices, body(): lax.all_gather(w_down, 'wsh', axis=0, tiled=True)  46.8 us
    reduce_scatter x1, waiting for transfers between devices, body(): lax.psum_scatter(terms[0].astype(jnp.bfloat16), 'wsh', scatter_dimension=...  43.5 us
    ppermute x2, waiting for transfers between devices, from_behind(): return lax.ppermute(value, axis, pairs)  25.5 us
    psum x1, blocking collectives, body(): lax.psum(owned[4].astype(jnp.bfloat16), 'seq').astype(jnp.float32)  22 us
  transfers between devices with their start and end apart: 13, of which 12 were waited for; matrix products, arithmetic and copies ran while one was open for 6% of the time, Pallas kernels for 0%

commit v1 on v0

--- a/solution.py
+++ b/solution.py
@@ -254,7 +254,9 @@
         ).astype(jnp.float32),
     )
     grads = (
-        lax.psum(owned[0].astype(jnp.bfloat16), "seq").astype(jnp.float32),
+        lax.all_gather(owned[0].astype(jnp.bfloat16), axis_name="seq")
+        .sum(axis=0)
+        .astype(jnp.float32),
         lax.psum(owned[1].astype(jnp.bfloat16), "seq").astype(jnp.float32),
         lax.psum(owned[2].astype(jnp.bfloat16), "seq").astype(jnp.float32),
         lax.psum(owned[3].astype(jnp.bfloat16), "seq").astype(jnp.float32),

time: 867 us -> 955 us (1.10)
  waiting for transfers between devices: 690 us -> 770 us
    all_gather x0 -> x1, waiting for transfers between devices: none -> 86.4 us  [body(): lax.all_gather(owned[0].astype(jnp.bfloat16), axis_name='seq').sum(axis=0)]
    reduce_scatter x1, waiting for transfers between devices: 6.06 us -> 35.3 us  [body(): lax.psum_scatter(terms[1].astype(jnp.bfloat16), 'wsh', scatter_dimension=...]
    reduce_scatter x1, waiting for transfers between devices: 43.5 us -> 15.4 us  [body(): lax.psum_scatter(terms[0].astype(jnp.bfloat16), 'wsh', scatter_dimension=...]
  transfers between devices with their start and end apart: 13 -> 14, of which waited for: 12 -> 13; matrix products, arithmetic and copies ran while one was open for 6% -> 6% of each run, Pallas kernels for 0% -> 0%
where the time goes in v1:
time: 955 us; the launch traced here: 954 us
  waiting for transfers between devices  770 us (81%)
  matrix products  65.3 us (7%)
  blocking collectives  46.6 us (5%)
  other arithmetic  34.3 us (4%)
  between operations  15.9 us (2%)
  local copies, waits for them, and re-layouts  15.7 us (2%)
    psum x1, waiting for transfers between devices, body(): lax.psum(owned[1].astype(jnp.bfloat16), 'seq').astype(jnp.float32)  215 us
    reduce_scatter x1, waiting for transfers between devices, body(): lax.psum_scatter(terms[2].astype(jnp.bfloat16), 'wsh', scatter_dimension=...  123 us
    all_gather x1, waiting for transfers between devices, body(): lax.all_gather(w_gate_up, 'wsh', axis=0, tiled=True)  95.5 us
    all_gather x1, waiting for transfers between devices, body(): lax.all_gather(owned[0].astype(jnp.bfloat16), axis_name='seq').sum(axis=0)  86.4 us
    reduce_scatter x1, waiting for transfers between devices, body(): lax.psum_scatter(terms[3].astype(jnp.bfloat16), 'wsh', scatter_dimension=...  72 us
    all_gather x1, waiting for transfers between devices, body(): lax.all_gather(w_down, 'wsh', axis=0, tiled=True)  46.8 us
    reduce_scatter x1, waiting for transfers between devices, body(): lax.psum_scatter(terms[1].astype(jnp.bfloat16), 'wsh', scatter_dimension=...  35.3 us
    ppermute x2, waiting for transfers between devices, from_behind(): return lax.ppermute(value, axis, pairs)  24.5 us
  transfers between devices with their start and end apart: 14, of which 13 were waited for; matrix products, arithmetic and copies ran while one was open for 6% of the time, Pallas kernels for 0%

profile of v1, /device:TPU:0, one launch (start us, length us, event | category | flops | bytes accessed | tf_op | source)
XLA Modules:
  0.0 953.8 jit_solution(15511145356568637675)
XLA Ops:
  10.1 6.2 all-gather.1
  16.4 5.3 all-gather.2
  22.6 20.4 %all-gather.9.cloned.1.call-done = bf16[1152,1536]{1,0:T(8,128)(2,1)} async-done(((bf16[288,1536]{1,0:T(8,128)(2,1)}), bf16[1152,1536]{1,0:T(8,128)(2,1)}) %all-gather.9.cloned.1.call-update) | async-done | bytes 3538960 | tf_op jit(solution)/shard_map/all_gather | solution.py:114
  43.0 2.7 fusion.50
  47.0 7.2 all_gather.36
  54.2 3.6 collective-permute-start
  58.8 10.5 %collective-permute-done = bf16[512,512]{1,0:T(8,128)(2,1)S(1)} collective-permute-done((bf16[512,512]{1,0:T(8,128)(2,1)S(1)}, bf16[512,512]{1,0:T(8,128)(2,1)S(1)}, u32[]{:S(2)}, u32[]{:S(2)}) %collective-permute-start) | collective-permute-done | bytes 524320 | tf_op jit(solution)/shard_map/ppermute | solution.py:14
  70.5 1.0 copy-done.16
  71.5 1.3 bitcast_convert_fusion
  72.8 2.7 multiply_reduce_fusion.6
  75.9 95.5 %all-gather.13.cloned.1.call-done = bf16[1152,6912]{1,0:T(8,128)(2,1)} async-done(((bf16[288,6912]{1,0:T(8,128)(2,1)}), bf16[1152,6912]{1,0:T(8,128)(2,1)}) %all-gather.13.cloned.1.call-update) | async-done | bytes 15925264 | tf_op jit(solution)/shard_map/all_gather | solution.py:116
  171.3 8.1 fusion.59
  179.4 1.8 copy-done
  181.8 46.8 %all-gather.15.cloned.1.call-done = bf16[1152,3456]{1,0:T(8,128)(2,1)} async-done(((bf16[288,3456]{1,0:T(8,128)(2,1)}), bf16[1152,3456]{1,0:T(8,128)(2,1)}) %all-gather.15.cloned.1.call-update) | async-done | bytes 7962640 | tf_op jit(solution)/shard_map/all_gather | solution.py:117
  228.6 6.0 multiply_reduce_fusion.4
  236.4 3.4 fusion.6
  239.8 12.7 %multiply_reduce_fusion = (bf16[1152]{0:T(1024)(128)(2,1)}, f32[128]{0:T(128)S(1)}, f32[128,1152]{1,0:T(8,128)}) fusion(f32[128,1152]{1,0:T(8,128)S(1)} %get-tuple-element.32, f32[128]{0:T(128)S(1)} %add_rsqrt_fusion.2, f32[1152]{0:T(1024)S(1)} %get-tuple-element.21, bf16[1152,6912]{1,0:T(8,128)(2,1)} %all-gather.13.cloned.1.call-done, ...), kind=kOutput, calls=%fused_computation.67 | convolution fusion | flops 2042854144 | bytes 18882304 | tf_op jit(solution)/shard_map/dot_general | solution.py:190
  252.6 2.3 multiply_reduce_fusion.1
  258.2 1.2 copy.113
  259.5 1.9 convolution_bitcast_fusion.2
  261.4 1.1 fusion.41
  262.6 1.1 fusion.9
  264.7 1.3 collective-permute-start.1
  266.5 14.1 %collective-permute-done.1 = bf16[512,512]{1,0:T(8,128)(2,1)S(1)} collective-permute-done((bf16[512,512]{1,0:T(8,128)(2,1)S(1)}, bf16[512,512]{1,0:T(8,128)(2,1)S(1)}, u32[]{:S(2)}, u32[]{:S(2)}) %collective-permute-start.1) | collective-permute-done | bytes 524320 | tf_op jit(solution)/shard_map/ppermute | solution.py:14
  281.7 1.4 broadcast_multiply_fusion
  284.2 19.2 %reduce-scatter.9.cloned.1.call-done = bf16[128,512]{1,0:T(8,128)(2,1)} async-done(((bf16[512,512]{1,0:T(8,128)(2,1)}), bf16[128,512]{1,0:T(8,128)(2,1)}) %reduce-scatter.9.cloned.1.call-update) | async-done | bytes 131088 | tf_op jit(solution)/shard_map/reduce_scatter | solution.py:209
  305.4 1.6 multiply_reduce_fusion.10
  308.1 3.0 convolution_convert_fusion.2
  312.2 2.2 convolution_convert_fusion.3
  315.3 6.0 convolution_convert_fusion.1
  321.5 1.1 copy-done.6
  322.9 8.1 convolution_convert_fusion
  331.9 3.4 fusion.35
  336.3 15.4 %reduce-scatter.11.cloned.1.call-done = bf16[288,1536]{1,0:T(8,128)(2,1)} async-done(((bf16[1152,1536]{1,0:T(8,128)(2,1)}), bf16[288,1536]{1,0:T(8,128)(2,1)}) %reduce-scatter.11.cloned.1.call-update) | async-done | bytes 884752 | tf_op jit(solution)/shard_map/reduce_scatter | solution.py:237
  351.7 35.3 %reduce-scatter.13.cloned.1.call-done = bf16[288,1024]{1,0:T(8,128)(2,1)} async-done(((bf16[1152,1024]{1,0:T(8,128)(2,1)}), bf16[288,1024]{1,0:T(8,128)(2,1)}) %reduce-scatter.13.cloned.1.call-update) | async-done | bytes 589840 | tf_op jit(solution)/shard_map/reduce_scatter | solution.py:240
  387.1 72.0 %reduce-scatter.17.cloned.1.call-done = bf16[288,3456]{1,0:T(8,128)(2,1)} async-done(((bf16[1152,3456]{1,0:T(8,128)(2,1)}), bf16[288,3456]{1,0:T(8,128)(2,1)}) %reduce-scatter.17.cloned.1.call-update) | async-done | bytes 1990672 | tf_op jit(solution)/shard_map/reduce_scatter | solution.py:246
  459.1 122.7 %reduce-scatter.15.cloned.1.call-done = bf16[288,6912]{1,0:T(8,128)(2,1)} async-done(((bf16[1152,6912]{1,0:T(8,128)(2,1)}), bf16[288,6912]{1,0:T(8,128)(2,1)}) %reduce-scatter.15.cloned.1.call-update) | async-done | bytes 3981328 | tf_op jit(solution)/shard_map/reduce_scatter | solution.py:243
  583.7 5.8 all-reduce
  589.6 1.0 fusion.34
  590.6 14.3 %reduce-scatter.19.cloned.1.call-done = bf16[288,4]{1,0:T(8,128)(2,1)} async-done(((bf16[1152,4]{1,0:T(8,128)(2,1)}), bf16[288,4]{1,0:T(8,128)(2,1)}) %reduce-scatter.19.cloned.1.call-update) | async-done | bytes 2320
  605.9 22.1 %all-reduce.1 = (bf16[4,288]{1,0:T(4,128)(2,1)S(1)}, bf16[128]{0:T(256)(128)(2,1)S(1)}) all-reduce(bf16[4,288]{1,0:T(4,128)(2,1)S(1)} %copy.125, bf16[128]{0:T(256)(128)(2,1)S(1)} %dynamic-slice.1), channel_id=1, replica_groups=mesh['seq'=8,'wsh'=4] {'seq'}, use_global_device_ids=true, to_apply=%region_27.28 | all-reduce | flops 1280 | bytes 5120 | tf_op jit(solution)/shard_map/psum | solution.py:263
  629.2 86.4 %all-gather.17.cloned.1.call-done = bf16[2304,1536]{1,0:T(8,128)(2,1)} async-done(((bf16[288,1536]{1,0:T(8,128)(2,1)}), bf16[2304,1536]{1,0:T(8,128)(2,1)}) %all-gather.17.cloned.1.call-update) | async-done | bytes 7077904 | tf_op jit(solution)/shard_map/all_gather | solution.py:257
  715.6 4.5 reduce_sum.196
  720.1 1.4 convert_element_type.148
  721.5 215.0 %all-reduce.5.cloned.1.call-done = (bf16[288,1024]{1,0:T(8,128)(2,1)}, bf16[288,6912]{1,0:T(8,128)(2,1)}, bf16[288,3456]{1,0:T(8,128)(2,1)}) async-done(((bf16[288,1024]{1,0:T(8,128)(2,1)}, bf16[288,6912]{1,0:T(8,128)(2,1)}, bf16[288,3456]{1,0:T(8,128)(2,1)}), (bf16[288,1024]{1,0:T(8,128)(2,1)}, bf16[288,6912]{1,0:T(8,128)(2,1)}, bf16[288,3456]{1,0:T(8,128)(2,1)})) %all-reduce.5.cloned.1.call-update) | async-done | bytes 6561808 | tf_op jit(solution)/shard_map/psum | solution.py:260
  936.5 2.2 convert_element_type.150
  938.7 6.0 convert_element_type.152
  944.7 2.2 convert_element_type.154
  (221 shorter events, 27.1 us)
Async XLA Ops:
  7.2 35.9 %all-gather.9.cloned.1.call-start = ((), (), s32[]{:S(2)}) async-start(), calls=%async_computation.6 | async-start | bytes 4423680 | tf_op jit(solution)/shard_map/all_gather | solution.py:114
  7.9 64.9 %all-gather.11.cloned.1.call-start = ((), (), s32[]{:S(2)}) async-start(), calls=%async_computation.7 | async-start | bytes 2949120 | tf_op jit(solution)/shard_map/all_gather | solution.py:115
  8.7 162.7 %all-gather.13.cloned.1.call-start = ((), (), s32[]{:S(2)}) async-start(), calls=%async_computation.8 | async-start | bytes 19906560 | tf_op jit(solution)/shard_map/all_gather | solution.py:116
  9.4 7.0 copy-start.58
  9.4 12.4 %copy-start.4 = (bf16[128,1152]{1,0:T(8,128)(2,1)S(1)}, bf16[128,1152]{1,0:T(8,128)(2,1)}, u32[]{:S(2)}) copy-start(bf16[128,1152]{1,0:T(8,128)(2,1)} %param.8) | copy-start | bytes 884740
  9.4 219.2 %all-gather.15.cloned.1.call-start = ((), (), s32[]{:S(2)}) async-start(), calls=%async_computation.9 | async-start | bytes 9953280 | tf_op jit(solution)/shard_map/all_gather | solution.py:117
  10.0 293.5 %reduce-scatter.9.cloned.1.call-start = ((), (), s32[]{:S(2)}) async-start(), calls=%async_computation.10 | async-start | bytes 655360 | tf_op jit(solution)/shard_map/reduce_scatter | solution.py:209
  22.0 23.8 %copy-start.52 = (f32[128]{0:T(128)}, f32[128]{0:T(128)S(1)}, u32[]{:S(2)}) copy-start(f32[128]{0:T(128)S(1)} %add_rsqrt_fusion.5) | copy-start | bytes 1540
  22.0 24.9 %copy-start.39 = (f32[2,1,128]{2,1,0:T(1,128)}, f32[2,1,128]{2,1,0:T(1,128)S(1)}, u32[]{:S(2)}) copy-start(f32[2,1,128]{2,1,0:T(1,128)S(1)} %get-tuple-element.48) | copy-start | bytes 3076
  22.0 36.2 %copy-start.46 = (f32[2,1,128]{2,1,0:T(1,128)}, f32[2,1,128]{2,1,0:T(1,128)S(1)}, u32[]{:S(2)}) copy-start(f32[2,1,128]{2,1,0:T(1,128)S(1)} %get-tuple-element.49) | copy-start | bytes 3076
  22.2 48.3 %copy-start.30 = (pred[128,640]{0,1:T(8,128)(4,1)}, pred[128,640]{0,1:T(8,128)(4,1)S(1)}, u32[]{:S(2)}) copy-start(pred[128,640]{0,1:T(8,128)(4,1)S(1)} %fusion.43) | copy-start | bytes 245764
  22.6 24.3 %copy-start.21 = (f32[128,128]{1,0:T(8,128)}, f32[128,128]{1,0:T(8,128)S(1)}, u32[]{:S(2)}) copy-start(f32[128,128]{1,0:T(8,128)S(1)} %get-tuple-element.50) | copy-start | bytes 196612
  22.6 24.3 %copy-start.28 = (f32[128,128]{1,0:T(8,128)}, f32[128,128]{1,0:T(8,128)S(1)}, u32[]{:S(2)}) copy-start(f32[128,128]{1,0:T(8,128)S(1)} %get-tuple-element.51) | copy-start | bytes 196612
  46.7 11.4 %copy-start.49 = (f32[128]{0:T(128)}, f32[128]{0:T(128)S(1)}, u32[]{:S(2)}) copy-start(f32[128]{0:T(128)S(1)} %add_rsqrt_fusion.4) | copy-start | bytes 1540
  54.2 15.0 %collective-permute-start = (bf16[512,512]{1,0:T(8,128)(2,1)S(1)}, bf16[512,512]{1,0:T(8,128)(2,1)S(1)}, u32[]{:S(2)}, u32[]{:S(2)}) collective-permute-start(bf16[512,512]{1,0:T(8,128)(2,1)S(1)} %all_gather.36), channel_id=1, source_target_pairs={{0,4},{4,8},{8,12},{12,16},{16,20},{20,24},{24,28},{1,5},{5,9},{9,... | collective-permute-start | bytes 1572872 | tf_op jit(solution)/shard_map/ppermute | solution.py:14
  58.0 12.1 %copy-start.20 = (f32[128,256]{0,1:T(8,128)}, f32[128,256]{0,1:T(8,128)S(1)}, u32[]{:S(2)}) copy-start(f32[128,256]{0,1:T(8,128)S(1)} %copy.91) | copy-start | bytes 393220
  58.8 11.7 %copy-start.25 = (bf16[128,4,256]{0,2,1:T(8,128)(2,1)}, bf16[128,4,256]{0,2,1:T(8,128)(2,1)S(1)}, u32[]{:S(2)}) copy-start(bf16[128,4,256]{0,2,1:T(8,128)(2,1)S(1)} %fusion.40) | copy-start | bytes 786436
  70.1 2.7 copy-start.14
  70.5 189.0 %copy-start.51 = (f32[4,128]{1,0:T(4,128)}, f32[4,128]{1,0:T(4,128)S(1)}, u32[]{:S(2)}) copy-start(f32[4,128]{1,0:T(4,128)S(1)} %log.8) | copy-start | bytes 6148
  72.8 3.0 copy-start.23
  75.8 176.7 %copy-start.41 = (f32[128]{0:T(128)}, f32[128]{0:T(128)S(1)}, u32[]{:S(2)}) copy-start(f32[128]{0:T(128)S(1)} %add_rsqrt_fusion.2) | copy-start | bytes 1540
  181.8 52.8 %copy-start.8 = (bf16[128,1152]{1,0:T(8,128)(2,1)S(1)}, bf16[128,1152]{1,0:T(8,128)(2,1)}, u32[]{:S(2)}) copy-start(bf16[128,1152]{1,0:T(8,128)(2,1)} %param.15) | copy-start | bytes 884740
  228.6 7.8 copy-start.1
  228.6 7.8 copy-start.3
  236.4 3.4 copy-start.12
  252.6 3.2 copy-start.2
  256.3 3.2 copy-start.31
  259.5 3.1 copy-start.15
  259.5 3.1 copy-start.17
  259.5 3.1 copy-start.27
  259.5 3.1 copy-start.32
  264.7 16.0 %collective-permute-start.1 = (bf16[512,512]{1,0:T(8,128)(2,1)S(1)}, bf16[512,512]{1,0:T(8,128)(2,1)S(1)}, u32[]{:S(2)}, u32[]{:S(2)}) collective-permute-start(bf16[512,512]{1,0:T(8,128)(2,1)S(1)} %slice.205), channel_id=1, source_target_pairs={{4,0},{8,4},{12,8},{16,12},{20,16},{24,20},{28,24},{5,1},{9,5},{13... | collective-permute-start | bytes 1572872 | tf_op jit(solution)/shard_map/ppermute | solution.py:14
  281.6 70.0 %reduce-scatter.11.cloned.1.call-start = ((), (), s32[]{:S(2)}) async-start(), calls=%async_computation.11 | async-start | bytes 4423680 | tf_op jit(solution)/shard_map/reduce_scatter | solution.py:237
  283.3 21.2 %copy-start.29 = (f32[128,128]{1,0:T(8,128)S(1)}, f32[128,128]{1,0:T(8,128)}, u32[]{:S(2)}) copy-start(f32[128,128]{1,0:T(8,128)} %copy-done.28) | copy-start | bytes 196612
  283.3 22.1 %copy-start.22 = (f32[128,128]{1,0:T(8,128)S(1)}, f32[128,128]{1,0:T(8,128)}, u32[]{:S(2)}) copy-start(f32[128,128]{1,0:T(8,128)} %copy-done.21) | copy-start | bytes 196612
  283.3 22.1 %copy-start.40 = (f32[2,1,128]{2,1,0:T(1,128)S(1)}, f32[2,1,128]{2,1,0:T(1,128)}, u32[]{:S(2)}) copy-start(f32[2,1,128]{2,1,0:T(1,128)} %copy-done.39) | copy-start | bytes 3076
  283.3 22.1 %copy-start.50 = (f32[128]{0:T(128)S(1)}, f32[128]{0:T(128)}, u32[]{:S(2)}) copy-start(f32[128]{0:T(128)} %copy-done.49) | copy-start | bytes 1540
  284.1 24.1 %copy-start.53 = (f32[128]{0:T(128)S(1)}, f32[128]{0:T(128)}, u32[]{:S(2)}) copy-start(f32[128]{0:T(128)} %copy-done.52) | copy-start | bytes 1540
  304.4 6.7 copy-start.33
  308.1 3.0 copy-start.35
  311.2 75.9 %reduce-scatter.13.cloned.1.call-start = ((), (), s32[]{:S(2)}) async-start(), calls=%async_computation.12 | async-start | bytes 2949120 | tf_op jit(solution)/shard_map/reduce_scatter | solution.py:240
  314.4 144.7 %reduce-scatter.17.cloned.1.call-start = ((), (), s32[]{:S(2)}) async-start(), calls=%async_computation.14 | async-start | bytes 9953280 | tf_op jit(solution)/shard_map/reduce_scatter | solution.py:246
  321.4 260.4 %reduce-scatter.15.cloned.1.call-start = ((), (), s32[]{:S(2)}) async-start(), calls=%async_computation.13 | async-start | bytes 19906560 | tf_op jit(solution)/shard_map/reduce_scatter | solution.py:243
  331.1 273.9 %reduce-scatter.19.cloned.1.call-start = ((), (), s32[]{:S(2)}) async-start(), calls=%async_computation.16 | async-start | bytes 368640
  336.2 379.3 %all-gather.17.cloned.1.call-start = ((), (), s32[]{:S(2)}) async-start(), calls=%async_computation.15 | async-start | bytes 7962624 | tf_op jit(solution)/shard_map/all_gather | solution.py:257
  351.7 584.8 %all-reduce.5.cloned.1.call-start = ((), (), s32[]{:S(2)}) async-start(), calls=%async_computation.17 | async-start | bytes 13123584 | tf_op jit(solution)/shard_map/psum | solution.py:260
  581.8 7.8 copy-start.54
  938.7 6.0 copy-start.11
  (26 other events, 30.6 us)
Sparse Core Ops, SparseCore 0:
  9.5 33.4 all-gather.8
  44.6 24.0 all-gather.10
  70.2 101.0 all-gather.12
  172.7 55.8 all-gather.14
  281.8 21.6 reduce-scatter.8
  311.3 40.3 reduce-scatter.10
  354.2 32.8 reduce-scatter.12
  390.2 68.8 reduce-scatter.16
  461.7 120.0 reduce-scatter.14
  584.7 20.2 reduce-scatter.18
  607.2 108.3 all-gather.16
  719.9 216.5 all-reduce.4
